TPU v7x, 128 devices: a whole 4x4x4 slice. The times are simulated.
128 devices in a mesh: req: 8 (over z, core), tok: 16 (over y, x).
Axes of the slice: x: 4, y: 4, z: 4, core: 2. Of those that a mesh axis runs over, the one named last changes fastest.
Arguments:
- draft_ids: int32 [32, 16], replicated, may hold values from 0 to 65535
- lengths: int32 [32], replicated, may hold values from 1 to 16384, as said below
- current_slot: int32 [32], replicated, may hold values from 0 to 31, as said below
- new_slot: int32 [32], replicated, may hold values from 0 to 31, as said below
- accepted: int32 [32], replicated, may hold values from 1 to 16, as said below
- embed_table: bfloat16 [65536, 3072], P(('req', 'tok')), may hold values from -6.5 to 6.5
- mixer_gain: float32 [3072], replicated, may hold values from 0.5 to 1.5
- query_weight: bfloat16 [3072, 768], replicated, may hold values from -0.3049512 to 0.3049512
- keyvalue_weight: bfloat16 [3072, 256], replicated, may hold values from -0.109375 to 0.109375
- key_cache: bfloat16 [32, 16384, 128], P('req', 'tok'), may hold values from -6 to 6
- value_cache: bfloat16 [32, 16384, 128], P('req', 'tok'), may hold values from -6 to 6
- attention_out: bfloat16 [768, 3072], P(None, 'tok'), may hold values from -0.21875 to 0.21875
- mamba_input: bfloat16 [3072, 2048], P(None, 'tok'), may hold values from -0.109375 to 0.109375
- mamba_gate: bfloat16 [3072, 2048], P(None, 'tok'), may hold values from -0.109375 to 0.109375
- state_proj: bfloat16 [3072, 512], replicated, may hold values from -0.02734375 to 0.02734375
- mamba_step: bfloat16 [3072, 16], P(None, 'tok'), may hold values from -0.109375 to 0.109375
- step_bias: float32 [16], P('tok'), may hold values from -4 to 0
- decay_log: float32 [16], P('tok'), may hold values from -2 to 1.5
- skip_gain: float32 [16], P('tok'), may hold values from 0.5 to 1.5
- states: float32 [32, 16, 128, 256], P('req', 'tok'), may hold values from -1.5 to 1.5
- mamba_out: bfloat16 [2048, 3072], P('tok'), may hold values from -0.125 to 0.125
- mlp_gain: float32 [3072], replicated, may hold values from 0.5 to 1.5
- gate_weight: bfloat16 [3072, 12288], P(None, ('req', 'tok')), may hold values from -0.109375 to 0.109375
- up_weight: bfloat16 [3072, 12288], P(None, ('req', 'tok')), may hold values from -0.109375 to 0.109375
- down_weight: bfloat16 [3072, 12288], P(None, ('req', 'tok')), may hold values from -0.0546875 to 0.0546875
Outputs:
- hidden_out: bfloat16 [512, 3072], P(('req', 'tok'))
- new_states: float32 [32, 16, 128, 256], P('req', 'tok')
Inputs may be any that keep to these rules, and one draw needn't show every extreme that they name: `lengths`: some request has exactly 16384 cached positions and some exactly one. `current_slot`: a permutation: each slot holds one request. `new_slot`: a permutation: each slot receives one request. `accepted`: some request accepts all 16 drafts and some exactly one.
All inputs are finite; a program needn't handle non-finite values.
Results may differ from a plain program's by a relative error of at most 0.02.
Values may be sent and summed in bfloat16 or wider, within the bound.
No kernel may reach another device: no remote copies, remote signals or barrier semaphores. Data moves between devices by JAX's collectives and lax.ppermute only.
A program may use at most 128 MiB of HBM per device.

v0:
```python
import jax
import jax.numpy as jnp
from jax import lax
from jax.sharding import PartitionSpec as P


def rms_rows(table_rows, norm_gain):
    values = table_rows.astype(jnp.float32)
    factor = lax.rsqrt(jnp.mean(values * values, axis=-1, keepdims=True) + 1e-05)
    return (values * factor * norm_gain).astype(jnp.bfloat16)


def inverse_of(mapping):
    places = jnp.arange(mapping.shape[0], dtype=jnp.int32)
    matches = mapping[None, :] == places[:, None]
    return jnp.sum(jnp.where(matches, places[None, :], 0), axis=1)


def recurrence(start_states, decay_rate, inputs, state_in, state_read, accept_count):

    def advance(state_pair, step_items):
        current, chosen = state_pair
        step_decay, step_input, step_in, step_read, step_index = step_items
        current = (
            step_decay[:, :, None, None] * current
            + step_input[..., None] * step_in[:, None, None, :]
        )
        readout = jnp.sum(current * step_read[:, None, None, :], axis=-1)
        chosen = jnp.where((accept_count == step_index + 1)[:, None, None, None], current, chosen)
        return ((current, chosen), readout)

    sequence = (
        jnp.swapaxes(decay_rate, 0, 1),
        jnp.swapaxes(inputs, 0, 1),
        jnp.swapaxes(state_in, 0, 1),
        jnp.swapaxes(state_read, 0, 1),
        jnp.arange(decay_rate.shape[1], dtype=jnp.int32),
    )
    (current, chosen), readouts = lax.scan(advance, (start_states, start_states), sequence)
    return (jnp.swapaxes(readouts, 0, 1), chosen)


def feed_units(block_rows, gate_cols, up_cols, down_cols):
    gate_part = jnp.dot(block_rows, gate_cols, preferred_element_type=jnp.float32)
    up_part = jnp.dot(block_rows, up_cols, preferred_element_type=jnp.float32)
    hidden = (jax.nn.silu(gate_part) * up_part).astype(jnp.bfloat16)
    return lax.dot_general(
        hidden, down_cols, (((1,), (1,)), ((), ())), preferred_element_type=jnp.float32
    )


def local(
    draft_ids,
    lengths,
    current_slot,
    new_slot,
    accepted,
    embed_table,
    mixer_gain,
    query_weight,
    keyvalue_weight,
    key_cache,
    value_cache,
    attention_out,
    mamba_input,
    mamba_gate,
    state_proj,
    mamba_step,
    step_bias,
    decay_log,
    skip_gain,
    states,
    mamba_out,
    mlp_gain,
    gate_weight,
    up_weight,
    down_weight,
):
    members = lax.axis_size("tok")
    group_index = lax.axis_index("req")
    member = lax.axis_index("tok")
    slots_dev, cache_dev, head_size = key_cache.shape
    draft_len = draft_ids.shape[1]
    group_tokens = slots_dev * draft_len
    vocab_dev = embed_table.shape[0]
    query_heads = query_weight.shape[1] // head_size
    heads_dev = step_bias.shape[0]
    mamba_head = mamba_input.shape[1] // heads_dev
    state_size = state_proj.shape[1] // 2
    slot_owner = inverse_of(current_slot)
    token_ids = jnp.take(draft_ids, slot_owner, axis=0).reshape(-1)
    vocab_start = (group_index * members + member) * vocab_dev
    wanted = token_ids - vocab_start
    inside = (wanted >= 0) & (wanted < vocab_dev)
    picked = jnp.take(embed_table, jnp.clip(wanted, 0, vocab_dev - 1), axis=0)
    embedded = lax.psum_scatter(
        jnp.where(inside[:, None], picked.astype(jnp.float32), 0.0),
        ("req", "tok"),
        scatter_dimension=0,
        tiled=True,
    ).astype(jnp.bfloat16)
    normed = rms_rows(embedded, mixer_gain)
    gathered = lax.all_gather(normed, "tok", axis=0, tiled=True)
    queries = jnp.dot(gathered, query_weight, preferred_element_type=jnp.float32).astype(
        jnp.bfloat16
    )
    queries = queries.reshape(slots_dev, draft_len, query_heads, head_size)
    keyvalue = jnp.dot(gathered, keyvalue_weight, preferred_element_type=jnp.float32).astype(
        jnp.bfloat16
    )
    keyvalue = keyvalue.reshape(slots_dev, draft_len, 2, head_size)
    local_owner = lax.dynamic_slice_in_dim(slot_owner, group_index * slots_dev, slots_dev)
    slot_length = jnp.take(lengths, local_owner)
    slot_accept = jnp.take(accepted, local_owner)
    score_scale = head_size ** (-0.5)
    positions = member * cache_dev + jnp.arange(cache_dev, dtype=jnp.int32)
    visible = (positions[None, :] < slot_length[:, None])[:, None, None, :]
    cache_scores = (
        jnp.einsum("sthd,spd->sthp", queries, key_cache, preferred_element_type=jnp.float32)
        * score_scale
    )
    local_max = jnp.max(jnp.where(visible, cache_scores, -1e30), axis=-1)
    cache_probs = jnp.where(visible, jnp.exp(cache_scores - local_max[..., None]), 0.0)
    local_total = jnp.sum(cache_probs, axis=-1)
    local_out = jnp.einsum(
        "sthp,spd->sthd",
        cache_probs.astype(jnp.bfloat16),
        value_cache,
        preferred_element_type=jnp.float32,
    )
    cache_max = lax.pmax(local_max, "tok")
    factor = jnp.exp(local_max - cache_max)
    cache_total, cache_out = (
        lax.psum((local_total * factor).astype(jnp.bfloat16), "tok").astype(jnp.float32),
        lax.psum((local_out * factor[..., None]).astype(jnp.bfloat16), "tok").astype(jnp.float32),
    )
    causal = (jnp.arange(draft_len)[None, :] <= jnp.arange(draft_len)[:, None])[None, :, None, :]
    draft_scores = (
        jnp.einsum("sthd,sud->sthu", queries, keyvalue[:, :, 0], preferred_element_type=jnp.float32)
        * score_scale
    )
    draft_max = jnp.max(jnp.where(causal, draft_scores, -1e30), axis=-1)
    joint_max = jnp.maximum(cache_max, draft_max)
    cache_factor = jnp.exp(cache_max - joint_max)
    draft_probs = jnp.where(causal, jnp.exp(draft_scores - joint_max[..., None]), 0.0)
    prob_total = cache_total * cache_factor + jnp.sum(draft_probs, axis=-1)
    summed = cache_out * cache_factor[..., None] + jnp.einsum(
        "sthu,sud->sthd",
        draft_probs.astype(jnp.bfloat16),
        keyvalue[:, :, 1],
        preferred_element_type=jnp.float32,
    )
    attended = (
        (summed / prob_total[..., None])
        .astype(jnp.bfloat16)
        .reshape(group_tokens, query_heads * head_size)
    )
    attn_proj = jnp.dot(attended, attention_out, preferred_element_type=jnp.float32)
    attn_rows = lax.all_to_all(
        attn_proj.astype(jnp.bfloat16), "tok", split_axis=0, concat_axis=1, tiled=True
    ).astype(attn_proj.dtype)
    mamba_x = jnp.dot(gathered, mamba_input, preferred_element_type=jnp.float32)
    mamba_x = mamba_x.reshape(slots_dev, draft_len, heads_dev, mamba_head)
    mamba_z = jnp.dot(gathered, mamba_gate, preferred_element_type=jnp.float32)
    mamba_z = mamba_z.reshape(slots_dev, draft_len, heads_dev, mamba_head)
    both_proj = jnp.dot(gathered, state_proj, preferred_element_type=jnp.float32)
    both_proj = both_proj.reshape(slots_dev, draft_len, 2, state_size)
    step_size = jax.nn.softplus(
        jnp.dot(gathered, mamba_step, preferred_element_type=jnp.float32) + step_bias
    ).reshape(slots_dev, draft_len, heads_dev)
    decay_rate = jnp.exp(-jnp.exp(decay_log) * step_size)
    readout, chosen = recurrence(
        states,
        decay_rate,
        step_size[..., None] * mamba_x,
        both_proj[:, :, 0],
        both_proj[:, :, 1],
        slot_accept,
    )
    readout = readout + skip_gain[None, None, :, None] * mamba_x
    gated = (
        (readout * jax.nn.silu(mamba_z))
        .astype(jnp.bfloat16)
        .reshape(group_tokens, heads_dev * mamba_head)
    )
    mamba_rows = lax.psum_scatter(
        jnp.dot(gated, mamba_out, preferred_element_type=jnp.float32).astype(jnp.bfloat16),
        "tok",
        scatter_dimension=0,
        tiled=True,
    ).astype(jnp.float32)
    mixed_rows = (embedded.astype(jnp.float32) + attn_rows + mamba_rows).astype(jnp.bfloat16)
    second = rms_rows(mixed_rows, mlp_gain)
    everything = lax.all_gather(second, ("req", "tok"), axis=0, tiled=True)
    mlp_rows = lax.psum_scatter(
        feed_units(everything, gate_weight, up_weight, down_weight),
        ("req", "tok"),
        scatter_dimension=0,
        tiled=True,
    )
    hidden_out = (mixed_rows.astype(jnp.float32) + mlp_rows).astype(jnp.bfloat16)
    every_state = lax.all_gather(chosen.astype(jnp.bfloat16), "req", axis=0, tiled=True).astype(
        chosen.dtype
    )
    incoming = inverse_of(new_slot)
    local_targets = lax.dynamic_slice_in_dim(incoming, group_index * slots_dev, slots_dev)
    sources = jnp.take(current_slot, local_targets)
    new_states = jnp.take(every_state, sources, axis=0)
    return (hidden_out, new_states)


def solution(mesh):
    return jax.shard_map(
        local,
        mesh=mesh,
        in_specs=(
            P(),
            P(),
            P(),
            P(),
            P(),
            P(("req", "tok"), None),
            P(),
            P(),
            P(),
            P("req", "tok", None),
            P("req", "tok", None),
            P(None, "tok"),
            P(None, "tok"),
            P(None, "tok"),
            P(),
            P(None, "tok"),
            P("tok"),
            P("tok"),
            P("tok"),
            P("req", "tok", None, None),
            P("tok", None),
            P(),
            P(None, ("req", "tok")),
            P(None, ("req", "tok")),
            P(None, ("req", "tok")),
        ),
        out_specs=(P(("req", "tok"), None), P("req", "tok", None, None)),
        check_vma=False,
    )
```

profile of v0, /device:TPU:1, one launch (start us, length us, event | category | flops | bytes accessed | tf_op | source)
XLA Modules:
  0.0 808.4 jit_solution(15467223869452533136)
XLA Ops:
  7.2 2.0 copy.142
  12.4 3.9 gather_fusion.1
  16.4 6.2 convert_select_fusion
  22.5 109.7 %all-reduce.11 = bf16[512,3072]{1,0:T(8,128)(2,1)} all-reduce(f32[512,3072]{1,0:T(8,128)} %convert_select_fusion), channel_id=2, replica_groups=mesh['req'=8,'tok'=16] {'req','tok'}, use_global_device_ids=true, to_apply=%region_1.2.clone | all-reduce | flops 1572864 | bytes 9437184
  133.7 19.8 %all-gather = bf16[16,4,3072]{2,1,0:T(4,128)(2,1)} all-gather(bf16[1,4,3072]{2,1,0:T(4,128)(2,1)S(1)} %fusion.44), channel_id=1, replica_groups=mesh['req'=8,'tok'=16] {'tok'}, dimensions={0}, use_global_device_ids=true | all-gather | bytes 417792 | tf_op jit(solution)/shard_map/all_gather | solution.py:103
  154.7 3.9 convolution_convert_fusion.1
  166.3 2.9 select_reduce_fusion
  169.2 57.9 %pmax.7 = f32[4,16,6]{1,2,0:T(8,128)} all-reduce(f32[4,16,6]{1,2,0:T(8,128)S(1)} %get-tuple-element.145), channel_id=1, replica_groups=mesh['req'=8,'tok'=16] {'tok'}, use_global_device_ids=true, to_apply=%region_4.6 | all-reduce | flops 384 | bytes 3072 | tf_op jit(solution)/shard_map/pmax | solution.py:131
  227.1 2.4 fusion.1
  229.5 2.4 convolution_convert_fusion.2
  234.8 3.2 fusion.54
  241.3 2.0 fusion.53
  255.5 165.3 %while.14 = (s32[]{:T(128)}, f32[4,1,128,256]{3,2,1,0:T(8,128)}, bf16[4,1,128,256]{3,2,1,0:T(8,128)(2,1)}, f32[16,4,1,128]{3,0,1,2:T(8,128)}, f32[16,4,1]{1,2,0:...) while((s32[]{:T(128)}, f32[4,1,128,256]{3,2,1,0:T(8,128)}, ...), condition=%wide.region_12.14_spmd, body=%wide.region_10.13_spmd.sunk | while | flops 785927 | bytes 2134257 | solution.py:39
  257.6 2.6 multiply_reduce_fusion.2
  268.0 2.6 multiply_reduce_fusion.2
  273.0 1.9 broadcast_select_fusion.4
  278.3 2.6 multiply_reduce_fusion.2
  283.3 1.9 broadcast_select_fusion.4
  288.7 2.6 multiply_reduce_fusion.2
  293.7 1.9 broadcast_select_fusion.4
  299.1 2.6 multiply_reduce_fusion.2
  309.4 2.6 multiply_reduce_fusion.2
  319.6 2.6 multiply_reduce_fusion.2
  330.0 2.6 multiply_reduce_fusion.2
  340.3 2.6 multiply_reduce_fusion.2
  350.6 2.6 multiply_reduce_fusion.2
  361.0 2.6 multiply_reduce_fusion.2
  371.3 2.6 multiply_reduce_fusion.2
  381.6 2.6 multiply_reduce_fusion.2
  391.9 2.6 multiply_reduce_fusion.2
  402.3 2.6 multiply_reduce_fusion.2
  412.6 2.6 multiply_reduce_fusion.2
  422.9 2.0 select_reduce_fusion.1
  425.7 2.2 convolution_convert_fusion
  428.6 2.8 fusion.5
  431.4 29.1 %psum.15 = bf16[4,16,6]{1,2,0:T(8,128)(2,1)S(1)} all-reduce(bf16[4,16,6]{1,2,0:T(8,128)(2,1)S(1)} %get-tuple-element.132), channel_id=1, replica_groups=mesh['req'=8,'tok'=16] {'tok'}, use_global_device_ids=true, to_apply=%region_8.10 | all-reduce | flops 384 | bytes 1536 | tf_op jit(solution)/shard_map/psum | solution.py:134
  462.2 68.0 %all-reduce.10.cloned.1.call-done = (bf16[4,16,6,128]{3,1,2,0:T(8,128)(2,1)}, bf16[64,3072]{1,0:T(8,128)(2,1)}) async-done(((bf16[4,16,6,128]{3,1,2,0:T(8,128)(2,1)}, bf16[64,3072]{1,0:T(8,128)(2,1)}), (bf16[4,16,6,128]{3,1,2,0:T(8,128)(2,1)}, bf16[64,3072]{1,0:T(8,128)(2,1)})) %all-reduce.10.cloned.1.call-update) | async-done | bytes 491536 | tf_op jit(solution)/shard_map/psum | solution.py:135
  532.4 3.8 all-to-all-start
  538.2 4.4 all-to-all-done
  546.1 66.2 %all-gather.7.cloned.1.call-done = bf16[128,4,3072]{2,1,0:T(4,128)(2,1)} async-done(((bf16[1,4,3072]{2,1,0:T(4,128)(2,1)}), bf16[128,4,3072]{2,1,0:T(4,128)(2,1)}) %all-gather.7.cloned.1.call-update) | async-done | bytes 3145744 | tf_op jit(solution)/shard_map/all_gather | solution.py:194
  612.3 6.0 reshape.403
  618.3 3.2 fusion.56
  621.4 6.9 fusion.7
  629.7 7.2 all-gather.5.cloned.1.call-done
  636.9 4.1 bitcast_convert_fusion
  641.0 3.6 gather_fusion.2
  644.6 1.9 fusion.15
  646.5 153.9 %all-reduce.8.cloned.1.call-done = f32[512,3072]{1,0:T(8,128)} async-done(((f32[512,3072]{1,0:T(8,128)}), f32[512,3072]{1,0:T(8,128)}) %all-reduce.8.cloned.1.call-update) | async-done | bytes 6291472
  (205 shorter events, 153.6 us)
Async XLA Ops:
  7.2 5.3 copy-start
  7.2 523.0 %all-reduce.10.cloned.1.call-start = ((), (), s32[]{:S(2)}) async-start(), calls=%async_computation.4 | async-start | bytes 983040 | tf_op jit(solution)/shard_map/psum | solution.py:135
  22.5 110.6 %copy-start.10 = (f32[3072]{0:T(1024)S(1)}, f32[3072]{0:T(1024)}, u32[]{:S(2)}) copy-start(f32[3072]{0:T(1024)} %param.35) | copy-start | bytes 36868
  133.1 0.6 copy-start.5
  153.5 6.7 copy-start.12
  153.6 8.6 %copy-start.1 = (s32[32]{0:T(128)S(1)}, s32[32]{0:T(128)}, u32[]{:S(2)}) copy-start(s32[32]{0:T(128)} %param.30) | copy-start | bytes 388
  154.7 8.6 %copy-start.2 = (s32[32]{0:T(128)S(1)}, s32[32]{0:T(128)}, u32[]{:S(2)}) copy-start(s32[32]{0:T(128)} %param.33) | copy-start | bytes 388
  165.7 0.6 copy-start.8
  422.2 39.3 %copy-start.7 = (f32[4,16,6]{1,2,0:T(8,128)S(1)}, f32[4,16,6]{1,2,0:T(8,128)}, u32[]{:S(2)}) copy-start(f32[4,16,6]{1,2,0:T(8,128)} %pmax.7) | copy-start | bytes 4612
  422.2 108.0 %copy-start.9 = (bf16[4,16,1,128]{3,2,1,0:T(2,128)(2,1)S(1)}, bf16[4,16,1,128]{3,2,1,0:T(2,128)(2,1)}, u32[]{:S(2)}) copy-start(bf16[4,16,1,128]{3,2,1,0:T(2,128)(2,1)} %get-tuple-element.140) | copy-start | bytes 49156
  425.7 105.8 %copy-start.4 = (bf16[768,192]{0,1:T(8,128)(2,1)S(1)}, bf16[768,192]{0,1:T(8,128)(2,1)}, u32[]{:S(2)}) copy-start(bf16[768,192]{0,1:T(8,128)(2,1)} %param.40) | copy-start | bytes 884740
  427.9 114.9 %copy-start.6 = (bf16[4,3072]{1,0:T(4,128)(2,1)S(1)}, bf16[4,3072]{1,0:T(4,128)(2,1)}, u32[]{:S(2)}) copy-start(bf16[4,3072]{1,0:T(4,128)(2,1)} %copy-done.5) | copy-start | bytes 73732
  532.4 10.3 %all-to-all-start = ((bf16[16,4,192]{2,1,0:T(4,128)(2,1)}), bf16[16,4,192]{2,1,0:T(4,128)(2,1)S(1)}, u32[]{:S(2)}, u32[]{:S(2)}) async-start(bf16[16,4,192]{2,1,0:T(4,128)(2,1)} %all_to_all.10), calls=%async_computation | async-start | bytes 65536 | tf_op jit(solution)/shard_map/all_to_all | solution.py:159
  536.2 76.1 %all-gather.7.cloned.1.call-start = ((), (), s32[]{:S(2)}) async-start(), calls=%async_computation.2 | async-start | bytes 3170304 | tf_op jit(solution)/shard_map/all_gather | solution.py:194
  545.2 91.8 %all-gather.5.cloned.1.call-start = ((), (), s32[]{:S(2)}) async-start(), calls=%async_computation.1 | async-start | bytes 2359296 | tf_op jit(solution)/shard_map/all_gather | solution.py:202
  545.9 254.5 %all-reduce.8.cloned.1.call-start = ((), (), s32[]{:S(2)}) async-start(), calls=%async_computation.3 | async-start | bytes 12582912
  628.3 0.7 copy-start.11
  628.3 0.7 copy-start.3
Sparse Core Ops, SparseCore 0:
  431.5 98.6 all-reduce.9
  545.3 66.9 all-gather.6
  614.1 22.7 all-gather.4
  642.4 157.9 all-reduce.7
where the time goes:
time: 814 us; the launch traced here: 808 us
  waiting for transfers between devices  300 us (37%)
  blocking collectives  216 us (27%)
  other arithmetic  113 us (14%)
  local copies, waits for them, and re-layouts  112 us (14%)
  matrix products  35.8 us (4%)
  between operations  16.7 us (2%)
  loops' own time  9.92 us (1%)
    unnamed x5, waiting for transfers between devices  155 us
    unnamed x1, blocking collectives  110 us
    psum x1, waiting for transfers between devices, local(): lax.psum((local_out * factor[..., None]).astype(jnp.bfloat16), 'tok')  68 us
    all_gather x1, waiting for transfers between devices, local(): everything = lax.all_gather(second, ('req', 'tok'), axis=0, tiled=True)  66.2 us
    pmax x1, blocking collectives, local(): cache_max = lax.pmax(local_max, 'tok')  57.9 us
    reduce_sum x16, other arithmetic, advance(): readout = jnp.sum(current * step_read[:, None, None, :], axis=-1)  41 us
    select_n x16, other arithmetic, advance(): jnp.where((accept_count == step_index + 1)[:, None, None, None], current,...  31 us
    dynamic_slice x32, local copies, waits for them, and re-layouts, recurrence(): lax.scan(advance, (start_states, start_states), sequence)  30.9 us
  transfers between devices with their start and end apart: 5, of which 5 were waited for; matrix products, arithmetic and copies ran while one was open for 4% of the time, Pallas kernels for 0%

commit v1 on v0

--- a/solution.py
+++ b/solution.py
@@ -100,7 +100,21 @@
         tiled=True,
     ).astype(jnp.bfloat16)
     normed = rms_rows(embedded, mixer_gain)
-    gathered = lax.all_gather(normed, "tok", axis=0, tiled=True)
+    ways, here, lap = (lax.axis_size("tok"), lax.axis_index("tok"), normed.shape[0])
+    lengths_2 = [n * ways if d == 0 else n for d, n in enumerate(normed.shape)]
+    full = lax.dynamic_update_slice_in_dim(
+        jnp.zeros(lengths_2, normed.dtype), normed, here * lap, axis=0
+    )
+    going_up = going_down = normed
+    for far in range(1, ways // 2 + 1):
+        going_up = lax.ppermute(going_up, "tok", [(d, (d + 1) % ways) for d in range(ways)])
+        full = lax.dynamic_update_slice_in_dim(full, going_up, (here - far) % ways * lap, axis=0)
+        if 2 * far < ways:
+            going_down = lax.ppermute(going_down, "tok", [(d, (d - 1) % ways) for d in range(ways)])
+            full = lax.dynamic_update_slice_in_dim(
+                full, going_down, (here + far) % ways * lap, axis=0
+            )
+    gathered = full
     queries = jnp.dot(gathered, query_weight, preferred_element_type=jnp.float32).astype(
         jnp.bfloat16
     )

time: 814 us -> 844 us (1.037)
  starting transfers between devices: 4.16 us -> 38.2 us
  blocking collectives: 216 us -> 194 us
  waiting for transfers between devices: 300 us -> 317 us
    ppermute x0 -> x15, starting transfers between devices: none -> 34.2 us  [the longest x7 33.1 us: local(): lax.ppermute(going_down, 'tok', [(d, (d - 1) % ways) for d in range(ways)])]
    all_gather x1 -> x0, blocking collectives: 19.8 us -> none  [local(): gathered = lax.all_gather(normed, 'tok', axis=0, tiled=True)]
    ppermute x0 -> x15, waiting for transfers between devices: none -> 11.1 us  [the longest x8 11 us: local(): lax.ppermute(going_up, 'tok', [(d, (d + 1) % ways) for d in range(ways)])]
  transfers between devices with their start and end apart: 5 -> 20, of which waited for: 5 -> 12; matrix products, arithmetic and copies ran while one was open for 4% -> 4% of each run, Pallas kernels for 0% -> 0%
where the time goes in v1:
time: 844 us; the launch traced here: 838 us
  waiting for transfers between devices  317 us (38%)
  blocking collectives  194 us (23%)
  other arithmetic  113 us (13%)
  local copies, waits for them, and re-layouts  111 us (13%)
  starting transfers between devices  38.2 us (5%)
  matrix products  35.9 us (4%)
  between operations  16.9 us (2%)
  loops' own time  10.1 us (1%)
    unnamed x5, waiting for transfers between devices  155 us
    unnamed x1, blocking collectives  110 us
    psum x1, waiting for transfers between devices, local(): lax.psum((local_out * factor[..., None]).astype(jnp.bfloat16), 'tok')  73.3 us
    all_gather x1, waiting for transfers between devices, local(): everything = lax.all_gather(second, ('req', 'tok'), axis=0, tiled=True)  66.3 us
    pmax x1, blocking collectives, local(): cache_max = lax.pmax(local_max, 'tok')  55.6 us
    reduce_sum x16, other arithmetic, advance(): readout = jnp.sum(current * step_read[:, None, None, :], axis=-1)  41 us
    ppermute x7, starting transfers between devices, local(): lax.ppermute(going_down, 'tok', [(d, (d - 1) % ways) for d in range(ways)])  33.1 us
    select_n x16, other arithmetic, advance(): jnp.where((accept_count == step_index + 1)[:, None, None, None], current,...  31.1 us
  transfers between devices with their start and end apart: 20, of which 12 were waited for; matrix products, arithmetic and copies ran while one was open for 4% of the time, Pallas kernels for 0%

profile of v1, /device:TPU:1, one launch (start us, length us, event | category | flops | bytes accessed | tf_op | source)
XLA Modules:
  0.0 837.5 jit_solution(12167083870177283595)
XLA Ops:
  12.3 3.9 gather_fusion.1
  16.2 6.2 convert_select_fusion
  22.4 109.7 %all-reduce.11 = bf16[512,3072]{1,0:T(8,128)(2,1)} all-reduce(f32[512,3072]{1,0:T(8,128)} %convert_select_fusion), channel_id=2, replica_groups=mesh['req'=8,'tok'=16] {'req','tok'}, use_global_device_ids=true, to_apply=%region_1.2.clone | all-reduce | flops 1572864 | bytes 9437184
  136.0 3.9 collective-permute-start.1
  149.4 4.8 collective-permute-start.3
  155.8 4.8 collective-permute-start.5
  161.8 4.8 collective-permute-start.7
  167.8 4.8 collective-permute-start.9
  173.8 5.1 collective-permute-start.11
  179.8 5.0 collective-permute-start.13
  185.8 5.9 collective-permute-done.14
  191.8 3.9 convolution_convert_fusion.1
  197.4 2.4 convolution_convert_fusion.2
  202.6 2.9 select_reduce_fusion
  205.5 55.6 %pmax.7 = f32[4,16,6]{1,2,0:T(8,128)} all-reduce(f32[4,16,6]{1,2,0:T(8,128)S(1)} %get-tuple-element.147), channel_id=1, replica_groups=mesh['req'=8,'tok'=16] {'tok'}, use_global_device_ids=true, to_apply=%region_4.6 | all-reduce | flops 384 | bytes 3072 | tf_op jit(solution)/shard_map/pmax | solution.py:145
  261.1 2.4 fusion.1
  263.5 3.2 fusion.54
  281.2 165.4 %while.14 = (s32[]{:T(128)}, f32[4,1,128,256]{3,2,1,0:T(8,128)}, bf16[4,1,128,256]{3,2,1,0:T(8,128)(2,1)}, f32[16,4,1,128]{3,0,1,2:T(8,128)}, f32[16,4,1]{1,2,0:...) while((s32[]{:T(128)}, f32[4,1,128,256]{3,2,1,0:T(8,128)}, ...), condition=%wide.region_12.14_spmd, body=%wide.region_10.13_spmd.sunk | while | flops 785927 | bytes 2134257 | solution.py:39
  283.2 2.6 multiply_reduce_fusion.2
  293.6 2.6 multiply_reduce_fusion.2
  303.9 2.6 multiply_reduce_fusion.2
  314.2 2.6 multiply_reduce_fusion.2
  324.6 2.6 multiply_reduce_fusion.2
  334.9 2.6 multiply_reduce_fusion.2
  345.2 2.6 multiply_reduce_fusion.2
  355.6 2.6 multiply_reduce_fusion.2
  365.9 2.6 multiply_reduce_fusion.2
  376.3 2.6 multiply_reduce_fusion.2
  386.6 2.6 multiply_reduce_fusion.2
  396.9 2.6 multiply_reduce_fusion.2
  407.3 2.6 multiply_reduce_fusion.2
  417.6 2.6 multiply_reduce_fusion.2
  427.9 2.6 multiply_reduce_fusion.2
  438.2 2.6 multiply_reduce_fusion.2
  450.1 2.1 convolution_convert_fusion
  453.0 2.8 fusion.5
  455.8 29.0 %psum.15 = bf16[4,16,6]{1,2,0:T(8,128)(2,1)S(1)} all-reduce(bf16[4,16,6]{1,2,0:T(8,128)(2,1)S(1)} %get-tuple-element.132), channel_id=1, replica_groups=mesh['req'=8,'tok'=16] {'tok'}, use_global_device_ids=true, to_apply=%region_8.10 | all-reduce | flops 384 | bytes 1536 | tf_op jit(solution)/shard_map/psum | solution.py:148
  484.9 73.3 %all-reduce.10.cloned.1.call-done = (bf16[4,16,6,128]{3,1,2,0:T(8,128)(2,1)}, bf16[64,3072]{1,0:T(8,128)(2,1)}) async-done(((bf16[4,16,6,128]{3,1,2,0:T(8,128)(2,1)}, bf16[64,3072]{1,0:T(8,128)(2,1)}), (bf16[4,16,6,128]{3,1,2,0:T(8,128)(2,1)}, bf16[64,3072]{1,0:T(8,128)(2,1)})) %all-reduce.10.cloned.1.call-update) | async-done | bytes 491536 | tf_op jit(solution)/shard_map/psum | solution.py:149
  561.2 3.8 all-to-all-start
  567.0 4.5 all-to-all-done
  574.8 66.3 %all-gather.6.cloned.1.call-done = bf16[128,4,3072]{2,1,0:T(4,128)(2,1)} async-done(((bf16[1,4,3072]{2,1,0:T(4,128)(2,1)}), bf16[128,4,3072]{2,1,0:T(4,128)(2,1)}) %all-gather.6.cloned.1.call-update) | async-done | bytes 3145744 | tf_op jit(solution)/shard_map/all_gather | solution.py:208
  641.2 5.9 reshape.401
  647.1 3.1 fusion.56
  650.2 7.0 fusion.7
  658.5 7.3 all-gather.4.cloned.1.call-done
  665.8 4.0 bitcast_convert_fusion
  669.9 3.6 gather_fusion.2
  675.4 154.1 %all-reduce.8.cloned.1.call-done = f32[512,3072]{1,0:T(8,128)} async-done(((f32[512,3072]{1,0:T(8,128)}), f32[512,3072]{1,0:T(8,128)}) %all-reduce.8.cloned.1.call-update) | async-done | bytes 6291472
  (245 shorter events, 173.3 us)
Async XLA Ops:
  7.2 5.1 copy-start
  7.2 551.1 %all-reduce.10.cloned.1.call-start = ((), (), s32[]{:S(2)}) async-start(), calls=%async_computation.4 | async-start | bytes 983040 | tf_op jit(solution)/shard_map/psum | solution.py:149
  10.0 0.5 copy-start.9
  22.4 117.5 %copy-start.10 = (s32[32]{0:T(128)S(1)}, s32[32]{0:T(128)}, u32[]{:S(2)}) copy-start(s32[32]{0:T(128)} %param.32) | copy-start | bytes 388
  22.4 118.8 %copy-start.1 = (s32[32]{0:T(128)S(1)}, s32[32]{0:T(128)}, u32[]{:S(2)}) copy-start(s32[32]{0:T(128)} %param.30) | copy-start | bytes 388
  22.4 120.0 %copy-start.2 = (s32[32]{0:T(128)S(1)}, s32[32]{0:T(128)}, u32[]{:S(2)}) copy-start(s32[32]{0:T(128)} %param.33) | copy-start | bytes 388
  135.1 14.2 %collective-permute-start = (bf16[4,3072]{1,0:T(4,128)(2,1)}, bf16[4,3072]{1,0:T(4,128)(2,1)}, u32[]{:S(2)}, u32[]{:S(2)}) collective-permute-start(bf16[4,3072]{1,0:T(4,128)(2,1)} %get-tuple-element.135), channel_id=1, source_target_pairs={{0,1},{1,2},{2,3},{3,4},{4,5},{5,6},{6,7},{7,8},{8,9},{9,10},{10,1... | collective-permute-start | bytes 73736 | tf_op jit(solution)/shard_map/ppermute | solution.py:110
  136.0 13.4 %collective-permute-start.1 = (bf16[4,3072]{1,0:T(4,128)(2,1)}, bf16[4,3072]{1,0:T(4,128)(2,1)}, u32[]{:S(2)}, u32[]{:S(2)}) collective-permute-start(bf16[4,3072]{1,0:T(4,128)(2,1)} %get-tuple-element.135), channel_id=1, source_target_pairs={{0,15},{1,0},{2,1},{3,2},{4,3},{5,4},{6,5},{7,6},{8,7},{9,8},{10,9... | collective-permute-start | bytes 73736 | tf_op jit(solution)/shard_map/ppermute | solution.py:113
  149.3 6.4 collective-permute-start.2
  149.4 6.4 collective-permute-start.3
  155.7 6.1 collective-permute-start.4
  155.8 6.0 collective-permute-start.5
  161.8 6.0 collective-permute-start.6
  161.8 6.0 collective-permute-start.7
  167.8 6.0 collective-permute-start.8
  167.8 6.0 collective-permute-start.9
  173.8 6.0 collective-permute-start.10
  173.8 6.1 collective-permute-start.11
  179.8 6.0 collective-permute-start.12
  179.8 6.0 collective-permute-start.13
  185.8 6.0 collective-permute-start.14
  447.9 36.9 %copy-start.7 = (pred[16,16]{0,1:T(8,128)(4,1)S(1)}, pred[16,16]{0,1:T(8,128)(4,1)}, u32[]{:S(2)}) copy-start(pred[16,16]{0,1:T(8,128)(4,1)} %iota_compare_fusion.2) | copy-start | bytes 772
  448.0 37.0 %copy-start.5 = (f32[4,16,6]{1,2,0:T(8,128)S(1)}, f32[4,16,6]{1,2,0:T(8,128)}, u32[]{:S(2)}) copy-start(f32[4,16,6]{1,2,0:T(8,128)} %pmax.7) | copy-start | bytes 4612
  448.0 110.3 %copy-start.6 = (bf16[4,16,1,128]{3,2,1,0:T(2,128)(2,1)S(1)}, bf16[4,16,1,128]{3,2,1,0:T(2,128)(2,1)}, u32[]{:S(2)}) copy-start(bf16[4,16,1,128]{3,2,1,0:T(2,128)(2,1)} %get-tuple-element.142) | copy-start | bytes 49156
  452.2 119.4 %copy-start.4 = (bf16[4,3072]{1,0:T(4,128)(2,1)S(1)}, bf16[4,3072]{1,0:T(4,128)(2,1)}, u32[]{:S(2)}) copy-start(bf16[4,3072]{1,0:T(4,128)(2,1)} %get-tuple-element.137) | copy-start | bytes 73732
  561.2 10.3 %all-to-all-start = ((bf16[16,4,192]{2,1,0:T(4,128)(2,1)}), bf16[16,4,192]{2,1,0:T(4,128)(2,1)S(1)}, u32[]{:S(2)}, u32[]{:S(2)}) async-start(bf16[16,4,192]{2,1,0:T(4,128)(2,1)} %all_to_all.10), calls=%async_computation | async-start | bytes 65536 | tf_op jit(solution)/shard_map/all_to_all | solution.py:173
  565.1 76.1 %all-gather.6.cloned.1.call-start = ((), (), s32[]{:S(2)}) async-start(), calls=%async_computation.2 | async-start | bytes 3170304 | tf_op jit(solution)/shard_map/all_gather | solution.py:208
  574.0 91.8 %all-gather.4.cloned.1.call-start = ((), (), s32[]{:S(2)}) async-start(), calls=%async_computation.1 | async-start | bytes 2359296 | tf_op jit(solution)/shard_map/all_gather | solution.py:216
  574.8 254.7 %all-reduce.8.cloned.1.call-start = ((), (), s32[]{:S(2)}) async-start(), calls=%async_computation.3 | async-start | bytes 12582912
  657.2 0.6 copy-start.8
  657.2 0.7 copy-start.3
Sparse Core Ops, SparseCore 0:
  455.9 102.2 all-reduce.9
  574.2 66.9 all-gather.5
  643.0 22.7 all-gather.3
  671.2 158.1 all-reduce.7
